TPU v7x, 512 devices: a whole 4x8x8 slice. The times are simulated.
512 devices in a mesh: cache: 64 (over x, z, core), rank: 8 (over y).
Axes of the slice: x: 4, y: 8, z: 8, core: 2. Of those that a mesh axis runs over, the one named last changes fastest.
Arguments:
- cand_rows: bfloat16 [64, 64, 4, 1024], P('cache', None, None, 'rank'), may hold values from -48 to 48
- listed: int32 [64], replicated, may hold values from 0 to 63, each once
- hist_len: int32 [64], P('cache'), may hold values from 768 to 3072, as said below
- block_mask: int32 [64, 24], P('cache'), may hold values 0 or 1
- hist_keys: bfloat16 [1, 64, 3072, 1024], P(None, 'cache', None, 'rank'), may hold values from -6 to 6
- hist_values: bfloat16 [1, 64, 3072, 1024], P(None, 'cache', None, 'rank'), may hold values from -6 to 6
- w_query: bfloat16 [1, 1024, 1024], P(None, None, 'rank'), may hold values from -0.1875 to 0.1875
- w_gate: bfloat16 [1, 1024, 1024], P(None, None, 'rank'), may hold values from -0.1875 to 0.1875
- w_out: bfloat16 [1, 1024, 1024], P(None, None, 'rank'), may hold values from -0.1875 to 0.1875
Outputs:
- ranked: bfloat16 [64, 64, 4, 1024], P('cache', None, None, 'rank')
Inputs may be any that keep to these rules, and one draw needn't show every extreme that they name: `hist_len`: some user has exactly 3072 history events. `listed`: each user id appears once.
All inputs are finite; a program needn't handle non-finite values. No bound on the sum of `block_mask` on one device may be relied on, other than what follows from the above.
Results may differ from a plain program's by a relative error of at most 0.0024.
Values may be sent and summed in bfloat16 or wider, within the bound.
A program may use at most 64 MiB of HBM per device.

v0:
```python
import jax
import jax.numpy as jnp
from jax import lax
from jax.sharding import PartitionSpec as P

D = 1024
HEADS = 8
BLOCK = 128
EPSILON = 1e-05
GROUP_BLOCKS = 4


def head_norm(values):
    centre = jnp.mean(values, axis=-1, keepdims=True)
    spread = jnp.mean(jnp.square(values - centre), axis=-1, keepdims=True)
    return (values - centre) * lax.rsqrt(spread + EPSILON)


def attend(queries, key_cache, value_cache, length, block_list, block_live, turn_count):
    head_size = queries.shape[-1]
    score_scale = head_size ** (-0.5)
    within = jnp.arange(BLOCK, dtype=jnp.int32)
    running = jnp.zeros(queries.shape, jnp.float32)

    def one_turn(turn_no, running):
        chosen = lax.dynamic_slice_in_dim(block_list, turn_no * GROUP_BLOCKS, GROUP_BLOCKS)
        chosen_live = lax.dynamic_slice_in_dim(block_live, turn_no * GROUP_BLOCKS, GROUP_BLOCKS)
        key_rows = jnp.take(key_cache, chosen, axis=0).reshape(
            GROUP_BLOCKS * BLOCK, key_cache.shape[2], head_size
        )
        value_rows = jnp.take(value_cache, chosen, axis=0).reshape(
            GROUP_BLOCKS * BLOCK, key_cache.shape[2], head_size
        )
        places = (chosen[:, None] * BLOCK + within[None, :]).reshape(GROUP_BLOCKS * BLOCK)
        live_mask = ((places < length) & jnp.repeat(chosen_live, BLOCK)).astype(jnp.float32)
        scores = (
            jnp.einsum("nkhe,the->nkht", queries, key_rows, preferred_element_type=jnp.float32)
            * score_scale
        )
        weights = (jax.nn.silu(scores) * live_mask).astype(jnp.bfloat16)
        return running + jnp.einsum(
            "nkht,the->nkhe", weights, value_rows, preferred_element_type=jnp.float32
        )

    return lax.fori_loop(0, turn_count, one_turn, running)


def finish(result):
    return lax.all_to_all(result, "cache", split_axis=0, concat_axis=1, tiled=True)


def on_device(
    cand_rows, listed, hist_len, block_mask, hist_keys, hist_values, w_query, w_gate, w_out
):
    head_size = D // HEADS
    local_width = w_query.shape[2]
    local_heads = local_width // head_size
    blocks_total = block_mask.shape[1]
    padded = -(-blocks_total // GROUP_BLOCKS) * GROUP_BLOCKS
    slot_of_user = jnp.argsort(listed)
    outgoing = jnp.take(cand_rows, slot_of_user, axis=1)
    length = hist_len[0]
    starts = jnp.arange(blocks_total, dtype=jnp.int32) * BLOCK
    usable = (block_mask[0] == 1) & (starts < length)
    filler = jnp.zeros((padded - blocks_total,), jnp.int32)
    block_list = jnp.concatenate([jnp.arange(blocks_total, dtype=jnp.int32), filler])
    block_live = jnp.concatenate([usable, filler > 0])
    turn_count = padded // GROUP_BLOCKS
    current = lax.all_to_all(outgoing, "cache", split_axis=1, concat_axis=0, tiled=True)
    whole_rows = lax.all_gather(current, "rank", axis=3, tiled=True)
    normed = head_norm(whole_rows.astype(jnp.float32)).astype(jnp.bfloat16)
    queries = jax.nn.silu(
        jnp.einsum("nukd,de->nuke", normed, w_query[0], preferred_element_type=jnp.float32)
    ).astype(jnp.bfloat16)
    gate_act = jax.nn.silu(
        jnp.einsum("nukd,de->nuke", normed, w_gate[0], preferred_element_type=jnp.float32)
    )
    split_shape = queries.shape[:3] + (local_heads, head_size)
    queries = queries.reshape(split_shape)
    length, block_list, block_live, turn_count = (length, block_list, block_live, turn_count)
    key_cache = hist_keys[0, 0].reshape(blocks_total, BLOCK, local_heads, head_size)
    value_cache = hist_values[0, 0].reshape(blocks_total, BLOCK, local_heads, head_size)
    attended_list = [
        attend(queries[:, 0], key_cache, value_cache, length, block_list, block_live, turn_count)
    ]
    attended = jnp.stack(attended_list, axis=1)
    hidden = (
        (head_norm(attended) * gate_act.reshape(split_shape))
        .reshape(queries.shape[:3] + (local_width,))
        .astype(jnp.bfloat16)
    )
    rows_in = w_out[0]
    projected = jnp.einsum(
        "nukd,de->nuke",
        lax.all_gather(hidden, "rank", axis=3, tiled=True),
        rows_in,
        preferred_element_type=jnp.float32,
    )
    current = (current.astype(jnp.float32) + projected).astype(jnp.bfloat16)
    returned = finish(current)
    return jnp.take(returned, listed, axis=1)


def solution(mesh):
    placed = (
        P("cache", None, None, "rank"),
        P(),
        P("cache"),
        P("cache", None),
        P(None, "cache", None, "rank"),
        P(None, "cache", None, "rank"),
        P(None, None, "rank"),
        P(None, None, "rank"),
        P(None, None, "rank"),
    )
    return jax.shard_map(
        on_device,
        mesh=mesh,
        in_specs=placed,
        out_specs=P("cache", None, None, "rank"),
        check_vma=False,
    )
```

profile of v0, /device:TPU:1, one launch (start us, length us, event | category | flops | bytes accessed | tf_op | source)
XLA Modules:
  0.0 122.2 jit_solution(12769290152046905703)
XLA Ops:
  0.7 2.0 %sort.17 = (s32[64]{0:T(128)}, s32[64]{0:T(128)S(1)}) sort(s32[64]{0:T(128)S(1)} %copy-done.4, s32[64]{0:T(128)S(1)} %iota.13), dimensions={0}, to_apply=%region_0.0 | sort | flops 384 | bytes 1024 | tf_op jit(solution)/shard_map/jit(argsort)/sort | solution.py:60
  2.8 1.5 %gather_fusion.2 = bf16[64,4,128]{2,1,0:T(4,128)(2,1)S(1)} fusion(bf16[64,4,128]{2,1,0:T(4,128)(2,1)} %bitcast.138, s32[1024]{0:T(1024)S(1)} %pad_clamp_fusion.2), kind=kCustom, calls=%fused_computation.clone | custom fusion | bytes 131328 | tf_op jit(solution)/shard_map/jit(_take)/gather | solution.py:61
  4.3 0.8 fusion.45
  5.0 14.8 %all-to-all-start = ((bf16[1,64,4,128]{3,2,0,1:T(4,128)(2,1)}), bf16[1,64,4,128]{3,2,0,1:T(4,128)(2,1)S(1)}, u32[]{:S(2)}, u32[]{:S(2)}) async-start(bf16[1,64,4,128]{3,2,0,1:T(4,128)(2,1)} %fusion.45), calls=%async_computation | async-start | bytes 131072 | tf_op jit(solution)/shard_map/all_to_all | solution.py:69
  21.2 8.5 %all-to-all-done = bf16[1,64,4,128]{3,2,0,1:T(4,128)(2,1)S(1)} async-done(((bf16[1,64,4,128]{3,2,0,1:T(4,128)(2,1)}), bf16[1,64,4,128]{3,2,0,1:T(4,128)(2,1)S(1)}, u32[]{:S(2)}, u32[]{:S(2)}) %all-to-all-start) | async-done | bytes 65568 | tf_op jit(solution)/shard_map/all_to_all | solution.py:69
  29.7 15.8 %all-gather = bf16[1,64,4,1024]{3,2,0,1:T(4,128)(2,1)S(1)} all-gather(bf16[1,64,4,128]{3,2,0,1:T(4,128)(2,1)S(1)} %all-to-all-done), channel_id=2, replica_groups=mesh['cache'=64,'rank'=8] {'rank'}, dimensions={3}, use_global_device_ids=true | all-gather | bytes 589824 | tf_op jit(solution)/shard_map/all_gather | solution.py:70
  47.0 29.7 %while.14 = (s32[]{:T(128)}, f32[64,4,1,128]{3,0,1,2:T(8,128)S(1)}, s32[24]{0:T(128)S(1)}, bf16[24,128,1,128]{3,1,0,2:T(8,128)(2,1)}, bf16[24,128,1,128]{3,1,0,2...) while((s32[]{:T(128)}, f32[64,4,1,128]{3,0,1,2:T(8,128)S(1)}, ...), condition=%wide.region_4.7_spmd.clone, body=%wide.region_3.6_spmd.clone.sunk | while | flops 68226080 | bytes 1646929 | solution.py:45
  47.1 1.7 %gather_fusion = bf16[4,128,128]{2,1,0:T(8,128)(2,1)S(1)} fusion(bf16[24,128,128]{2,1,0:T(8,128)(2,1)} %bitcast.136, s32[1024]{0:T(1024)S(1)} %pad_clamp_fusion.4), kind=kCustom, calls=%fused_computation.3.clone.clone.1 | custom fusion | bytes 262160 | tf_op jit(solution)/shard_map/while/body/eval_jaxpr/jit(_take)/gather | solution.py:28
  48.8 1.7 %gather_fusion.1 = bf16[4,128,128]{2,1,0:T(8,128)(2,1)S(1)} fusion(bf16[24,128,128]{2,1,0:T(8,128)(2,1)} %bitcast.134, s32[1024]{0:T(1024)S(1)} %pad_clamp_fusion.4), kind=kCustom, calls=%fused_computation.1.clone.clone.1 | custom fusion | bytes 262160 | tf_op jit(solution)/shard_map/while/body/eval_jaxpr/jit(_take)/gather | solution.py:31
  50.8 0.7 convert_bitcast_fusion.3
  52.0 1.7 %gather_fusion = bf16[4,128,128]{2,1,0:T(8,128)(2,1)S(1)} fusion(bf16[24,128,128]{2,1,0:T(8,128)(2,1)} %bitcast.136, s32[1024]{0:T(1024)S(1)} %pad_clamp_fusion.4), kind=kCustom, calls=%fused_computation.3.clone.clone.1 | custom fusion | bytes 262160 | tf_op jit(solution)/shard_map/while/body/eval_jaxpr/jit(_take)/gather | solution.py:28
  53.7 1.7 %gather_fusion.1 = bf16[4,128,128]{2,1,0:T(8,128)(2,1)S(1)} fusion(bf16[24,128,128]{2,1,0:T(8,128)(2,1)} %bitcast.134, s32[1024]{0:T(1024)S(1)} %pad_clamp_fusion.4), kind=kCustom, calls=%fused_computation.1.clone.clone.1 | custom fusion | bytes 262160 | tf_op jit(solution)/shard_map/while/body/eval_jaxpr/jit(_take)/gather | solution.py:31
  57.0 1.7 %gather_fusion = bf16[4,128,128]{2,1,0:T(8,128)(2,1)S(1)} fusion(bf16[24,128,128]{2,1,0:T(8,128)(2,1)} %bitcast.136, s32[1024]{0:T(1024)S(1)} %pad_clamp_fusion.4), kind=kCustom, calls=%fused_computation.3.clone.clone.1 | custom fusion | bytes 262160 | tf_op jit(solution)/shard_map/while/body/eval_jaxpr/jit(_take)/gather | solution.py:28
  58.7 1.7 %gather_fusion.1 = bf16[4,128,128]{2,1,0:T(8,128)(2,1)S(1)} fusion(bf16[24,128,128]{2,1,0:T(8,128)(2,1)} %bitcast.134, s32[1024]{0:T(1024)S(1)} %pad_clamp_fusion.4), kind=kCustom, calls=%fused_computation.1.clone.clone.1 | custom fusion | bytes 262160 | tf_op jit(solution)/shard_map/while/body/eval_jaxpr/jit(_take)/gather | solution.py:31
  61.9 1.7 %gather_fusion = bf16[4,128,128]{2,1,0:T(8,128)(2,1)S(1)} fusion(bf16[24,128,128]{2,1,0:T(8,128)(2,1)} %bitcast.136, s32[1024]{0:T(1024)S(1)} %pad_clamp_fusion.4), kind=kCustom, calls=%fused_computation.3.clone.clone.1 | custom fusion | bytes 262160 | tf_op jit(solution)/shard_map/while/body/eval_jaxpr/jit(_take)/gather | solution.py:28
  63.6 1.7 %gather_fusion.1 = bf16[4,128,128]{2,1,0:T(8,128)(2,1)S(1)} fusion(bf16[24,128,128]{2,1,0:T(8,128)(2,1)} %bitcast.134, s32[1024]{0:T(1024)S(1)} %pad_clamp_fusion.4), kind=kCustom, calls=%fused_computation.1.clone.clone.1 | custom fusion | bytes 262160 | tf_op jit(solution)/shard_map/while/body/eval_jaxpr/jit(_take)/gather | solution.py:31
  66.9 1.7 %gather_fusion = bf16[4,128,128]{2,1,0:T(8,128)(2,1)S(1)} fusion(bf16[24,128,128]{2,1,0:T(8,128)(2,1)} %bitcast.136, s32[1024]{0:T(1024)S(1)} %pad_clamp_fusion.4), kind=kCustom, calls=%fused_computation.3.clone.clone.1 | custom fusion | bytes 262160 | tf_op jit(solution)/shard_map/while/body/eval_jaxpr/jit(_take)/gather | solution.py:28
  68.6 1.7 %gather_fusion.1 = bf16[4,128,128]{2,1,0:T(8,128)(2,1)S(1)} fusion(bf16[24,128,128]{2,1,0:T(8,128)(2,1)} %bitcast.134, s32[1024]{0:T(1024)S(1)} %pad_clamp_fusion.4), kind=kCustom, calls=%fused_computation.1.clone.clone.1 | custom fusion | bytes 262160 | tf_op jit(solution)/shard_map/while/body/eval_jaxpr/jit(_take)/gather | solution.py:31
  71.8 1.7 %gather_fusion = bf16[4,128,128]{2,1,0:T(8,128)(2,1)S(1)} fusion(bf16[24,128,128]{2,1,0:T(8,128)(2,1)} %bitcast.136, s32[1024]{0:T(1024)S(1)} %pad_clamp_fusion.4), kind=kCustom, calls=%fused_computation.3.clone.clone.1 | custom fusion | bytes 262160 | tf_op jit(solution)/shard_map/while/body/eval_jaxpr/jit(_take)/gather | solution.py:28
  73.6 1.7 %gather_fusion.1 = bf16[4,128,128]{2,1,0:T(8,128)(2,1)S(1)} fusion(bf16[24,128,128]{2,1,0:T(8,128)(2,1)} %bitcast.134, s32[1024]{0:T(1024)S(1)} %pad_clamp_fusion.4), kind=kCustom, calls=%fused_computation.1.clone.clone.1 | custom fusion | bytes 262160 | tf_op jit(solution)/shard_map/while/body/eval_jaxpr/jit(_take)/gather | solution.py:31
  78.0 19.5 %all-gather.1 = bf16[64,4,1024]{2,0,1:T(8,128)(2,1)S(1)} all-gather(bf16[64,4,128]{2,0,1:T(8,128)(2,1)S(1)} %fusion.31), channel_id=3, replica_groups=mesh['cache'=64,'rank'=8] {'rank'}, dimensions={2}, use_global_device_ids=true | all-gather | bytes 589824 | tf_op jit(solution)/shard_map/all_gather | solution.py:95
  98.5 12.4 %all-to-all-start.1 = ((bf16[64,1,4,128]{3,2,1,0:T(4,128)(2,1)}), bf16[64,1,4,128]{3,2,1,0:T(4,128)(2,1)S(1)}, u32[]{:S(2)}, u32[]{:S(2)}) async-start(bf16[64,1,4,128]{3,2,1,0:T(4,128)(2,1)} %copy.46), calls=%async_computation.1 | async-start | bytes 131072 | tf_op jit(solution)/shard_map/all_to_all | solution.py:49
  110.9 9.9 %all-to-all-done.1 = bf16[64,1,4,128]{3,2,1,0:T(4,128)(2,1)S(1)} async-done(((bf16[64,1,4,128]{3,2,1,0:T(4,128)(2,1)}), bf16[64,1,4,128]{3,2,1,0:T(4,128)(2,1)S(1)}, u32[]{:S(2)}, u32[]{:S(2)}) %all-to-all-start.1) | async-done | bytes 65568 | tf_op jit(solution)/shard_map/all_to_all | solution.py:49
  121.4 0.8 bitcast_select_fusion.2
  (75 shorter events, 14.0 us)
Async XLA Ops:
  0.0 46.6 %copy-start = (bf16[1,1024,128]{2,1,0:T(8,128)(2,1)S(1)}, bf16[1,1024,128]{2,1,0:T(8,128)(2,1)}, u32[]{:S(2)}) copy-start(bf16[1,1024,128]{2,1,0:T(8,128)(2,1)} %param.21) | copy-start | bytes 786436
  0.0 0.7 copy-start.4
  5.0 24.6 %all-to-all-start = ((bf16[1,64,4,128]{3,2,0,1:T(4,128)(2,1)}), bf16[1,64,4,128]{3,2,0,1:T(4,128)(2,1)S(1)}, u32[]{:S(2)}, u32[]{:S(2)}) async-start(bf16[1,64,4,128]{3,2,0,1:T(4,128)(2,1)} %fusion.45), calls=%async_computation | async-start | bytes 131072 | tf_op jit(solution)/shard_map/all_to_all | solution.py:69
  20.5 0.7 copy-start.3
  76.7 1.0 copy-start.2
  78.0 19.5 %copy-start.1 = (bf16[1,1024,128]{2,1,0:T(8,128)(2,1)S(1)}, bf16[1,1024,128]{2,1,0:T(8,128)(2,1)}, u32[]{:S(2)}) copy-start(bf16[1,1024,128]{2,1,0:T(8,128)(2,1)} %param.23) | copy-start | bytes 786436
  98.5 22.3 %all-to-all-start.1 = ((bf16[64,1,4,128]{3,2,1,0:T(4,128)(2,1)}), bf16[64,1,4,128]{3,2,1,0:T(4,128)(2,1)S(1)}, u32[]{:S(2)}, u32[]{:S(2)}) async-start(bf16[64,1,4,128]{3,2,1,0:T(4,128)(2,1)} %copy.46), calls=%async_computation.1 | async-start | bytes 131072 | tf_op jit(solution)/shard_map/all_to_all | solution.py:49
where the time goes:
time: 123 us; the launch traced here: 122 us
  blocking collectives  35.3 us (29%)
  starting transfers between devices  27.3 us (22%)
  local copies, waits for them, and re-layouts  25.8 us (21%)
  waiting for transfers between devices  18.3 us (15%)
  other arithmetic  10.9 us (9%)
  matrix products  3.56 us (3%)
    all_gather x1, blocking collectives, on_device(): lax.all_gather(hidden, 'rank', axis=3, tiled=True)  19.5 us
    all_gather x1, blocking collectives, on_device(): whole_rows = lax.all_gather(current, 'rank', axis=3, tiled=True)  15.8 us
    all_to_all x1, starting transfers between devices, on_device(): lax.all_to_all(outgoing, 'cache', split_axis=1, concat_axis=0, tiled=True)  14.8 us
    all_to_all x1, starting transfers between devices, finish(): lax.all_to_all(result, 'cache', split_axis=0, concat_axis=1, tiled=True)  12.4 us
    gather x6, local copies, waits for them, and re-layouts, one_turn(): jnp.take(key_cache, chosen, axis=0)  10.2 us
    gather x6, local copies, waits for them, and re-layouts, one_turn(): jnp.take(value_cache, chosen, axis=0)  10.2 us
    all_to_all x1, waiting for transfers between devices, finish(): lax.all_to_all(result, 'cache', split_axis=0, concat_axis=1, tiled=True)  9.87 us
    all_to_all x1, waiting for transfers between devices, on_device(): lax.all_to_all(outgoing, 'cache', split_axis=1, concat_axis=0, tiled=True)  8.45 us
  transfers between devices with their start and end apart: 2, of which 2 were waited for; matrix products, arithmetic and copies ran while one was open for 0% of the time, Pallas kernels for 0%

commit v1 on v0

--- a/solution.py
+++ b/solution.py
@@ -92,7 +92,9 @@
     rows_in = w_out[0]
     projected = jnp.einsum(
         "nukd,de->nuke",
-        lax.all_gather(hidden, "rank", axis=3, tiled=True),
+        jnp.concatenate(
+            lax.all_to_all(jnp.stack([hidden] * lax.axis_size("rank")), "rank", 0, 0), axis=3
+        ),
         rows_in,
         preferred_element_type=jnp.float32,
     )

time: 123 us -> 121 us (0.984)
  blocking collectives: 35.3 us -> 15.8 us
  waiting for transfers between devices: 18.3 us -> 31.4 us
  local copies, waits for them, and re-layouts: 25.8 us -> 27.9 us
  starting transfers between devices: 27.3 us -> 29.1 us
    all_gather x1 -> x0, blocking collectives: 19.5 us -> none  [on_device(): lax.all_gather(hidden, 'rank', axis=3, tiled=True)]
    all_to_all x0 -> x1, waiting for transfers between devices: none -> 13.1 us  [on_device(): lax.all_to_all(jnp.stack([hidden] * lax.axis_size('rank')), 'rank', 0, 0)]
    all_to_all x0 -> x1, starting transfers between devices: none -> 4.89 us  [on_device(): lax.all_to_all(jnp.stack([hidden] * lax.axis_size('rank')), 'rank', 0, 0)]
    all_to_all x1, starting transfers between devices: 12.4 us -> 9.4 us  [finish(): lax.all_to_all(result, 'cache', split_axis=0, concat_axis=1, tiled=True)]
  transfers between devices with their start and end apart: 2 -> 3, of which waited for: 2 -> 3; matrix products, arithmetic and copies ran while one was open for 0% -> 0% of each run, Pallas kernels for 0% -> 0%
where the time goes in v1:
time: 121 us; the launch traced here: 120 us
  waiting for transfers between devices  31.4 us (26%)
  starting transfers between devices  29.1 us (24%)
  local copies, waits for them, and re-layouts  27.9 us (23%)
  blocking collectives  15.8 us (13%)
  other arithmetic  10.9 us (9%)
  matrix products  3.57 us (3%)
    all_gather x1, blocking collectives, on_device(): whole_rows = lax.all_gather(current, 'rank', axis=3, tiled=True)  15.8 us
    all_to_all x1, starting transfers between devices, on_device(): lax.all_to_all(outgoing, 'cache', split_axis=1, concat_axis=0, tiled=True)  14.8 us
    all_to_all x1, waiting for transfers between devices, on_device(): lax.all_to_all(jnp.stack([hidden] * lax.axis_size('rank')), 'rank', 0, 0)  13.1 us
    gather x6, local copies, waits for them, and re-layouts, one_turn(): jnp.take(value_cache, chosen, axis=0)  10.2 us
    gather x6, local copies, waits for them, and re-layouts, one_turn(): jnp.take(key_cache, chosen, axis=0)  10.2 us
    all_to_all x1, waiting for transfers between devices, finish(): lax.all_to_all(result, 'cache', split_axis=0, concat_axis=1, tiled=True)  9.87 us
    all_to_all x1, starting transfers between devices, finish(): lax.all_to_all(result, 'cache', split_axis=0, concat_axis=1, tiled=True)  9.4 us
    all_to_all x1, waiting for transfers between devices, on_device(): lax.all_to_all(outgoing, 'cache', split_axis=1, concat_axis=0, tiled=True)  8.46 us
  transfers between devices with their start and end apart: 3, of which 3 were waited for; matrix products, arithmetic and copies ran while one was open for 0% of the time, Pallas kernels for 0%

profile of v1, /device:TPU:1, one launch (start us, length us, event | category | flops | bytes accessed | tf_op | source)
XLA Modules:
  0.0 119.9 jit_solution(5113821395280949704)
XLA Ops:
  0.7 2.0 %sort.17 = (s32[64]{0:T(128)}, s32[64]{0:T(128)S(1)}) sort(s32[64]{0:T(128)S(1)} %copy-done.4, s32[64]{0:T(128)S(1)} %iota.13), dimensions={0}, to_apply=%region_0.0 | sort | flops 384 | bytes 1024 | tf_op jit(solution)/shard_map/jit(argsort)/sort | solution.py:60
  2.8 1.5 %gather_fusion.2 = bf16[64,4,128]{2,1,0:T(4,128)(2,1)S(1)} fusion(bf16[64,4,128]{2,1,0:T(4,128)(2,1)} %bitcast.144, s32[1024]{0:T(1024)S(1)} %pad_clamp_fusion.2), kind=kCustom, calls=%fused_computation.clone | custom fusion | bytes 131328 | tf_op jit(solution)/shard_map/jit(_take)/gather | solution.py:61
  4.3 0.8 fusion.45
  5.0 14.8 %all-to-all-start = ((bf16[1,64,4,128]{3,2,0,1:T(4,128)(2,1)}), bf16[1,64,4,128]{3,2,0,1:T(4,128)(2,1)S(1)}, u32[]{:S(2)}, u32[]{:S(2)}) async-start(bf16[1,64,4,128]{3,2,0,1:T(4,128)(2,1)} %fusion.45), calls=%async_computation | async-start | bytes 131072 | tf_op jit(solution)/shard_map/all_to_all | solution.py:69
  21.2 8.5 %all-to-all-done = bf16[1,64,4,128]{3,2,0,1:T(4,128)(2,1)S(1)} async-done(((bf16[1,64,4,128]{3,2,0,1:T(4,128)(2,1)}), bf16[1,64,4,128]{3,2,0,1:T(4,128)(2,1)S(1)}, u32[]{:S(2)}, u32[]{:S(2)}) %all-to-all-start) | async-done | bytes 65568 | tf_op jit(solution)/shard_map/all_to_all | solution.py:69
  29.7 15.8 %all-gather = bf16[1,64,4,1024]{3,2,0,1:T(4,128)(2,1)S(1)} all-gather(bf16[1,64,4,128]{3,2,0,1:T(4,128)(2,1)S(1)} %all-to-all-done), channel_id=2, replica_groups=mesh['cache'=64,'rank'=8] {'rank'}, dimensions={3}, use_global_device_ids=true | all-gather | bytes 589824 | tf_op jit(solution)/shard_map/all_gather | solution.py:70
  47.0 29.7 %while.14 = (s32[]{:T(128)}, f32[64,4,1,128]{3,0,1,2:T(8,128)S(1)}, s32[24]{0:T(128)S(1)}, bf16[24,128,1,128]{3,1,0,2:T(8,128)(2,1)}, bf16[24,128,1,128]{3,1,0,2...) while((s32[]{:T(128)}, f32[64,4,1,128]{3,0,1,2:T(8,128)S(1)}, ...), condition=%wide.region_4.7_spmd.clone, body=%wide.region_3.6_spmd.clone.sunk | while | flops 68226080 | bytes 1646929 | solution.py:45
  47.1 1.7 %gather_fusion = bf16[4,128,128]{2,1,0:T(8,128)(2,1)S(1)} fusion(bf16[24,128,128]{2,1,0:T(8,128)(2,1)} %bitcast.142, s32[1024]{0:T(1024)S(1)} %pad_clamp_fusion.4), kind=kCustom, calls=%fused_computation.3.clone.clone.1 | custom fusion | bytes 262160 | tf_op jit(solution)/shard_map/while/body/eval_jaxpr/jit(_take)/gather | solution.py:28
  48.8 1.7 %gather_fusion.1 = bf16[4,128,128]{2,1,0:T(8,128)(2,1)S(1)} fusion(bf16[24,128,128]{2,1,0:T(8,128)(2,1)} %bitcast.140, s32[1024]{0:T(1024)S(1)} %pad_clamp_fusion.4), kind=kCustom, calls=%fused_computation.1.clone.clone.1 | custom fusion | bytes 262160 | tf_op jit(solution)/shard_map/while/body/eval_jaxpr/jit(_take)/gather | solution.py:31
  52.0 1.7 %gather_fusion = bf16[4,128,128]{2,1,0:T(8,128)(2,1)S(1)} fusion(bf16[24,128,128]{2,1,0:T(8,128)(2,1)} %bitcast.142, s32[1024]{0:T(1024)S(1)} %pad_clamp_fusion.4), kind=kCustom, calls=%fused_computation.3.clone.clone.1 | custom fusion | bytes 262160 | tf_op jit(solution)/shard_map/while/body/eval_jaxpr/jit(_take)/gather | solution.py:28
  53.7 1.7 %gather_fusion.1 = bf16[4,128,128]{2,1,0:T(8,128)(2,1)S(1)} fusion(bf16[24,128,128]{2,1,0:T(8,128)(2,1)} %bitcast.140, s32[1024]{0:T(1024)S(1)} %pad_clamp_fusion.4), kind=kCustom, calls=%fused_computation.1.clone.clone.1 | custom fusion | bytes 262160 | tf_op jit(solution)/shard_map/while/body/eval_jaxpr/jit(_take)/gather | solution.py:31
  57.0 1.7 %gather_fusion = bf16[4,128,128]{2,1,0:T(8,128)(2,1)S(1)} fusion(bf16[24,128,128]{2,1,0:T(8,128)(2,1)} %bitcast.142, s32[1024]{0:T(1024)S(1)} %pad_clamp_fusion.4), kind=kCustom, calls=%fused_computation.3.clone.clone.1 | custom fusion | bytes 262160 | tf_op jit(solution)/shard_map/while/body/eval_jaxpr/jit(_take)/gather | solution.py:28
  58.7 1.7 %gather_fusion.1 = bf16[4,128,128]{2,1,0:T(8,128)(2,1)S(1)} fusion(bf16[24,128,128]{2,1,0:T(8,128)(2,1)} %bitcast.140, s32[1024]{0:T(1024)S(1)} %pad_clamp_fusion.4), kind=kCustom, calls=%fused_computation.1.clone.clone.1 | custom fusion | bytes 262160 | tf_op jit(solution)/shard_map/while/body/eval_jaxpr/jit(_take)/gather | solution.py:31
  61.9 1.7 %gather_fusion = bf16[4,128,128]{2,1,0:T(8,128)(2,1)S(1)} fusion(bf16[24,128,128]{2,1,0:T(8,128)(2,1)} %bitcast.142, s32[1024]{0:T(1024)S(1)} %pad_clamp_fusion.4), kind=kCustom, calls=%fused_computation.3.clone.clone.1 | custom fusion | bytes 262160 | tf_op jit(solution)/shard_map/while/body/eval_jaxpr/jit(_take)/gather | solution.py:28
  63.7 1.7 %gather_fusion.1 = bf16[4,128,128]{2,1,0:T(8,128)(2,1)S(1)} fusion(bf16[24,128,128]{2,1,0:T(8,128)(2,1)} %bitcast.140, s32[1024]{0:T(1024)S(1)} %pad_clamp_fusion.4), kind=kCustom, calls=%fused_computation.1.clone.clone.1 | custom fusion | bytes 262160 | tf_op jit(solution)/shard_map/while/body/eval_jaxpr/jit(_take)/gather | solution.py:31
  66.9 1.7 %gather_fusion = bf16[4,128,128]{2,1,0:T(8,128)(2,1)S(1)} fusion(bf16[24,128,128]{2,1,0:T(8,128)(2,1)} %bitcast.142, s32[1024]{0:T(1024)S(1)} %pad_clamp_fusion.4), kind=kCustom, calls=%fused_computation.3.clone.clone.1 | custom fusion | bytes 262160 | tf_op jit(solution)/shard_map/while/body/eval_jaxpr/jit(_take)/gather | solution.py:28
  68.6 1.7 %gather_fusion.1 = bf16[4,128,128]{2,1,0:T(8,128)(2,1)S(1)} fusion(bf16[24,128,128]{2,1,0:T(8,128)(2,1)} %bitcast.140, s32[1024]{0:T(1024)S(1)} %pad_clamp_fusion.4), kind=kCustom, calls=%fused_computation.1.clone.clone.1 | custom fusion | bytes 262160 | tf_op jit(solution)/shard_map/while/body/eval_jaxpr/jit(_take)/gather | solution.py:31
  71.9 1.7 %gather_fusion = bf16[4,128,128]{2,1,0:T(8,128)(2,1)S(1)} fusion(bf16[24,128,128]{2,1,0:T(8,128)(2,1)} %bitcast.142, s32[1024]{0:T(1024)S(1)} %pad_clamp_fusion.4), kind=kCustom, calls=%fused_computation.3.clone.clone.1 | custom fusion | bytes 262160 | tf_op jit(solution)/shard_map/while/body/eval_jaxpr/jit(_take)/gather | solution.py:28
  73.6 1.7 %gather_fusion.1 = bf16[4,128,128]{2,1,0:T(8,128)(2,1)S(1)} fusion(bf16[24,128,128]{2,1,0:T(8,128)(2,1)} %bitcast.140, s32[1024]{0:T(1024)S(1)} %pad_clamp_fusion.4), kind=kCustom, calls=%fused_computation.1.clone.clone.1 | custom fusion | bytes 262160 | tf_op jit(solution)/shard_map/while/body/eval_jaxpr/jit(_take)/gather | solution.py:31
  78.0 0.9 stack.5
  78.9 4.9 %all-to-all-start.1 = ((bf16[8,64,1,4,128]{4,1,3,2,0:T(8,128)(2,1)}), bf16[8,64,1,4,128]{4,1,3,2,0:T(8,128)(2,1)S(1)}, u32[]{:S(2)}, u32[]{:S(2)}) async-start(bf16[8,64,1,4,128]{4,1,3,2,0:T(8,128)(2,1)} %stack.5), calls=%async_computation.1 | async-start | bytes 1048576 | tf_op jit(solution)/shard_map/all_to_all | solution.py:96
  83.8 13.1 %all-to-all-done.1 = bf16[8,64,1,4,128]{4,1,3,2,0:T(8,128)(2,1)S(1)} async-done(((bf16[8,64,1,4,128]{4,1,3,2,0:T(8,128)(2,1)}), bf16[8,64,1,4,128]{4,1,3,2,0:T(8,128)(2,1)S(1)}, u32[]{:S(2)}, u32[]{:S(2)}) %all-to-all-start.1) | async-done | bytes 524320 | tf_op jit(solution)/shard_map/all_to_all | solution.py:96
  99.2 9.4 %all-to-all-start.2 = ((bf16[64,1,4,128]{3,2,1,0:T(4,128)(2,1)}), bf16[64,1,4,128]{3,2,1,0:T(4,128)(2,1)S(1)}, u32[]{:S(2)}, u32[]{:S(2)}) async-start(bf16[64,1,4,128]{3,2,1,0:T(4,128)(2,1)} %copy.50), calls=%async_computation.2 | async-start | bytes 131072 | tf_op jit(solution)/shard_map/all_to_all | solution.py:49
  108.6 9.9 %all-to-all-done.2 = bf16[64,1,4,128]{3,2,1,0:T(4,128)(2,1)S(1)} async-done(((bf16[64,1,4,128]{3,2,1,0:T(4,128)(2,1)}), bf16[64,1,4,128]{3,2,1,0:T(4,128)(2,1)S(1)}, u32[]{:S(2)}, u32[]{:S(2)}) %all-to-all-start.2) | async-done | bytes 65568 | tf_op jit(solution)/shard_map/all_to_all | solution.py:49
  (79 shorter events, 16.7 us)
Async XLA Ops:
  0.0 46.6 %copy-start = (bf16[1,1024,128]{2,1,0:T(8,128)(2,1)S(1)}, bf16[1,1024,128]{2,1,0:T(8,128)(2,1)}, u32[]{:S(2)}) copy-start(bf16[1,1024,128]{2,1,0:T(8,128)(2,1)} %param.21) | copy-start | bytes 786436
  0.0 0.7 copy-start.4
  5.0 24.6 %all-to-all-start = ((bf16[1,64,4,128]{3,2,0,1:T(4,128)(2,1)}), bf16[1,64,4,128]{3,2,0,1:T(4,128)(2,1)S(1)}, u32[]{:S(2)}, u32[]{:S(2)}) async-start(bf16[1,64,4,128]{3,2,0,1:T(4,128)(2,1)} %fusion.45), calls=%async_computation | async-start | bytes 131072 | tf_op jit(solution)/shard_map/all_to_all | solution.py:69
  20.5 0.7 copy-start.3
  76.7 1.0 copy-start.2
  78.9 18.0 %all-to-all-start.1 = ((bf16[8,64,1,4,128]{4,1,3,2,0:T(8,128)(2,1)}), bf16[8,64,1,4,128]{4,1,3,2,0:T(8,128)(2,1)S(1)}, u32[]{:S(2)}, u32[]{:S(2)}) async-start(bf16[8,64,1,4,128]{4,1,3,2,0:T(8,128)(2,1)} %stack.5), calls=%async_computation.1 | async-start | bytes 1048576 | tf_op jit(solution)/shard_map/all_to_all | solution.py:96
  97.2 1.0 copy-start.1
  99.2 19.3 %all-to-all-start.2 = ((bf16[64,1,4,128]{3,2,1,0:T(4,128)(2,1)}), bf16[64,1,4,128]{3,2,1,0:T(4,128)(2,1)S(1)}, u32[]{:S(2)}, u32[]{:S(2)}) async-start(bf16[64,1,4,128]{3,2,1,0:T(4,128)(2,1)} %copy.50), calls=%async_computation.2 | async-start | bytes 131072 | tf_op jit(solution)/shard_map/all_to_all | solution.py:49
